TPU v7x, 32 devices: a whole 2x2x4 slice. The times are simulated.
32 devices in a mesh: dev: 8 (over z, x), ma: 4 (over y, core).
Axes of the slice: x: 2, y: 2, z: 4, core: 2. Of those that a mesh axis runs over, the one named last changes fastest.
Arguments:
- inputs: bfloat16 [8192, 2048], P('ma', 'dev'), may hold values from -6 to 6
- cotangent: bfloat16 [8192, 2048], P('ma', 'dev'), may hold values from -6 to 6
- factors: bfloat16 [4, 64, 16384], P(None, 'ma', 'dev'), may hold values from -0.5 to 0.5
- exponents: int32 [4, 64], P(None, 'ma'), may hold values from -6 to -4
- error_buffer: bfloat16 [8, 4, 64, 16384], P('dev', None, 'ma'), may hold values from -96 to 96
Outputs:
- output: bfloat16 [8192, 2048], P('ma', 'dev')
- input_grad: bfloat16 [8192, 2048], P('ma', 'dev')
- grad_mean: float32 [4, 64, 16384], P(None, 'ma', 'dev')
- new_error: bfloat16 [8, 4, 64, 16384], P('dev', None, 'ma')
All inputs are finite; a program needn't handle non-finite values.
Results may differ from a plain program's by a relative error of at most 0.0057.
Values may be sent and summed in bfloat16 or wider, within the bound.
A program may use at most 64 MiB of HBM per device.

v0:
```python
import jax
import jax.numpy as jnp
from jax import lax
from jax.sharding import PartitionSpec as P

B = 128
code_limit = 127.0


def regroup(stacked):
    groups = lax.axis_size("ma")
    count, local_blocks, width, tok_count = stacked.shape
    folded = stacked.reshape(
        count, local_blocks, width // (groups * local_blocks), groups, local_blocks, tok_count
    )
    shaped = jnp.transpose(folded, (0, 4, 2, 3, 1, 5))
    arrived = lax.all_to_all(shaped, "ma", split_axis=3, concat_axis=3, tiled=True)
    return arrived.reshape(count, local_blocks, width, tok_count)


def block_forward(weights, values):
    return jnp.einsum("ncd,nct->ndt", weights, values, preferred_element_type=jnp.float32)


def block_backward(weights, values):
    return jnp.einsum("ncd,ndt->nct", weights, values, preferred_element_type=jnp.float32)


def outer_sum(left, right):
    return jnp.einsum("nct,ndt->ncd", left, right, preferred_element_type=jnp.float32)


def quantize(gradients, error_part, exponent_part):
    totals = gradients.reshape(gradients.shape[:-2] + (-1,)) + error_part.astype(jnp.float32)
    scale_inverse = jnp.left_shift(jnp.ones_like(exponent_part), -exponent_part).astype(
        jnp.float32
    )[..., None]
    code_values = jnp.clip(totals * scale_inverse, -code_limit, code_limit)
    return (code_values, (totals - code_values / scale_inverse).astype(jnp.bfloat16), scale_inverse)


def body(inputs, cotangent, factors, exponents, error_buffer):
    local_blocks = factors.shape[1]
    tok_count = inputs.shape[1]
    group_count = lax.axis_size("dev")
    gathered = lax.all_gather(factors, "dev", axis=2, tiled=True)
    matrices = gathered.reshape(gathered.shape[0], local_blocks, B, B)
    block_in = inputs.reshape(local_blocks, B, tok_count)
    block_cot = cotangent.reshape(local_blocks, B, tok_count)
    first_out = block_forward(matrices[0], block_in).astype(jnp.bfloat16)
    mixed_one = regroup(first_out[None])[0]
    second_out = block_forward(matrices[1], mixed_one).astype(jnp.bfloat16)
    pre_gelu = regroup(second_out[None])[0]
    hidden_wide, gelu_back = jax.vjp(jax.nn.gelu, pre_gelu.astype(jnp.float32))
    hidden = hidden_wide.astype(jnp.bfloat16)
    third_out = block_forward(matrices[2], hidden).astype(jnp.bfloat16)
    mixed_two = regroup(third_out[None])[0]
    fourth_out = block_forward(matrices[3], mixed_two).astype(jnp.bfloat16)
    returned = regroup(fourth_out[None])[0]
    output = (block_in.astype(jnp.float32) + returned.astype(jnp.float32)).astype(jnp.bfloat16)
    back_four = regroup(block_cot[None])[0]
    d_mixed_two = block_backward(matrices[3], back_four).astype(jnp.bfloat16)
    gradient_three = outer_sum(mixed_two, back_four)
    d_third = regroup(d_mixed_two[None])[0]
    d_pre = gelu_back(block_backward(matrices[2], d_third))[0].astype(jnp.bfloat16)
    gradient_two = outer_sum(hidden, d_third)
    d_second = regroup(d_pre[None])[0]
    d_mixed_one = block_backward(matrices[1], d_second).astype(jnp.bfloat16)
    gradient_one = outer_sum(mixed_one, d_second)
    d_first = regroup(d_mixed_one[None])[0]
    input_grad = (block_cot.astype(jnp.float32) + block_backward(matrices[0], d_first)).astype(
        jnp.bfloat16
    )
    gradient_zero = outer_sum(block_in, d_first)
    gradients = jnp.stack([gradient_zero, gradient_one, gradient_two, gradient_three])
    code_values, new_part, scale_inverse = quantize(gradients, error_buffer[0], exponents)
    summed = lax.psum_scatter(code_values, "dev", scatter_dimension=2, tiled=True)
    grad_mean = summed / scale_inverse / group_count
    new_error = new_part[None]
    return (
        output.reshape(local_blocks * B, tok_count),
        input_grad.reshape(local_blocks * B, tok_count),
        grad_mean,
        new_error,
    )


def solution(mesh):
    in_specs = (
        P("ma", "dev"),
        P("ma", "dev"),
        P(None, "ma", "dev"),
        P(None, "ma"),
        P("dev", None, "ma", None),
    )
    out_specs = (P("ma", "dev"), P("ma", "dev"), P(None, "ma", "dev"), P("dev", None, "ma", None))
    return jax.shard_map(body, mesh=mesh, in_specs=in_specs, out_specs=out_specs, check_vma=False)
```

profile of v0, /device:TPU:0, one launch (start us, length us, event | category | flops | bytes accessed | tf_op | source)
XLA Modules:
  0.0 293.5 jit_solution(14815720484470332092)
XLA Ops:
  7.9 2.8 copy.67
  10.7 4.3 %all-to-all-start.4 = ((bf16[1,16,2,4,16,256]{5,4,2,1,0,3:T(8,128)(2,1)}), bf16[1,16,2,4,16,256]{5,4,2,1,0,3:T(8,128)(2,1)S(1)}, u32[]{:S(2)}, u32[]{:S(2)}) async-start(bf16[1,16,2,4,16,256]{5,4,2,1,0,3:T(8,128)(2,1)} %copy.67), calls=%async_computation.4 | async-start | bytes 2097152 | tf_op jit(solution)/shard_map/all_to_all | solution.py:17
  14.9 47.0 %all-gather.2.cloned.1.call-done = bf16[4,16,16384]{2,1,0:T(8,128)(2,1)} async-done(((bf16[4,16,2048]{2,1,0:T(8,128)(2,1)}), bf16[4,16,16384]{2,1,0:T(8,128)(2,1)}) %all-gather.2.cloned.1.call-update) | async-done | bytes 2097168 | tf_op jit(solution)/shard_map/all_gather | solution.py:46
  62.0 2.7 slice_bitcast_fusion
  67.2 4.2 %all-to-all-start = ((bf16[1,16,2,4,16,256]{5,1,2,4,0,3:T(8,128)(2,1)}), bf16[1,16,2,4,16,256]{5,1,2,4,0,3:T(8,128)(2,1)}, u32[]{:S(2)}, u32[]{:S(2)}) async-start(bf16[1,16,2,4,16,256]{5,1,2,4,0,3:T(8,128)(2,1)} %bitcast.115), calls=%async_computation | async-start | bytes 2097152 | tf_op jit(solution)/shard_map/all_to_all | solution.py:17
  74.9 11.0 %all-to-all-done = bf16[1,16,2,4,16,256]{5,1,2,4,0,3:T(8,128)(2,1)} async-done(((bf16[1,16,2,4,16,256]{5,1,2,4,0,3:T(8,128)(2,1)}), bf16[1,16,2,4,16,256]{5,1,2,4,0,3:T(8,128)(2,1)}, u32[]{:S(2)}, u32[]{:S(2)}) %all-to-all-start) | async-done | bytes 1048608 | tf_op jit(solution)/shard_map/all_to_all | solution.py:17
  85.9 4.2 %all-to-all-start.5 = ((bf16[1,16,2,4,16,256]{5,1,2,4,0,3:T(8,128)(2,1)}), bf16[1,16,2,4,16,256]{5,1,2,4,0,3:T(8,128)(2,1)}, u32[]{:S(2)}, u32[]{:S(2)}) async-start(bf16[1,16,2,4,16,256]{5,1,2,4,0,3:T(8,128)(2,1)} %bitcast.111), calls=%async_computation.5 | async-start | bytes 2097152 | tf_op jit(solution)/shard_map/all_to_all | solution.py:17
  90.3 2.0 copy.57
  93.9 10.8 %all-to-all-done.5 = bf16[1,16,2,4,16,256]{5,1,2,4,0,3:T(8,128)(2,1)} async-done(((bf16[1,16,2,4,16,256]{5,1,2,4,0,3:T(8,128)(2,1)}), bf16[1,16,2,4,16,256]{5,1,2,4,0,3:T(8,128)(2,1)}, u32[]{:S(2)}, u32[]{:S(2)}) %all-to-all-start.5) | async-done | bytes 1048608 | tf_op jit(solution)/shard_map/all_to_all | solution.py:17
  104.7 4.2 %all-to-all-start.1 = ((bf16[1,16,2,4,16,256]{5,1,2,4,0,3:T(8,128)(2,1)}), bf16[1,16,2,4,16,256]{5,1,2,4,0,3:T(8,128)(2,1)}, u32[]{:S(2)}, u32[]{:S(2)}) async-start(bf16[1,16,2,4,16,256]{5,1,2,4,0,3:T(8,128)(2,1)} %bitcast.138), calls=%async_computation.1 | async-start | bytes 2097152 | tf_op jit(solution)/shard_map/all_to_all | solution.py:17
  108.9 1.9 copy.83
  110.9 2.8 copy.70
  113.6 9.8 %all-to-all-done.1 = bf16[1,16,2,4,16,256]{5,1,2,4,0,3:T(8,128)(2,1)} async-done(((bf16[1,16,2,4,16,256]{5,1,2,4,0,3:T(8,128)(2,1)}), bf16[1,16,2,4,16,256]{5,1,2,4,0,3:T(8,128)(2,1)}, u32[]{:S(2)}, u32[]{:S(2)}) %all-to-all-start.1) | async-done | bytes 1048608 | tf_op jit(solution)/shard_map/all_to_all | solution.py:17
  123.4 2.0 copy.60
  125.4 1.6 fusion.9
  128.1 4.2 %all-to-all-start.6 = ((bf16[1,16,2,4,16,256]{5,1,2,4,0,3:T(8,128)(2,1)}), bf16[1,16,2,4,16,256]{5,1,2,4,0,3:T(8,128)(2,1)}, u32[]{:S(2)}, u32[]{:S(2)}) async-start(bf16[1,16,2,4,16,256]{5,1,2,4,0,3:T(8,128)(2,1)} %bitcast.140), calls=%async_computation.6 | async-start | bytes 2097152 | tf_op jit(solution)/shard_map/all_to_all | solution.py:17
  132.4 2.6 convolution_convert_fusion.3
  136.1 10.8 %all-to-all-done.6 = bf16[1,16,2,4,16,256]{5,1,2,4,0,3:T(8,128)(2,1)} async-done(((bf16[1,16,2,4,16,256]{5,1,2,4,0,3:T(8,128)(2,1)}), bf16[1,16,2,4,16,256]{5,1,2,4,0,3:T(8,128)(2,1)}, u32[]{:S(2)}, u32[]{:S(2)}) %all-to-all-start.6) | async-done | bytes 1048608 | tf_op jit(solution)/shard_map/all_to_all | solution.py:17
  146.8 4.2 %all-to-all-start.2 = ((bf16[1,16,2,4,16,256]{5,1,2,4,0,3:T(8,128)(2,1)}), bf16[1,16,2,4,16,256]{5,1,2,4,0,3:T(8,128)(2,1)}, u32[]{:S(2)}, u32[]{:S(2)}) async-start(bf16[1,16,2,4,16,256]{5,1,2,4,0,3:T(8,128)(2,1)} %bitcast.137), calls=%async_computation.2 | async-start | bytes 2097152 | tf_op jit(solution)/shard_map/all_to_all | solution.py:17
  151.1 1.9 copy.72
  154.4 1.1 copy.92
  155.6 10.0 %all-to-all-done.2 = bf16[1,16,2,4,16,256]{5,1,2,4,0,3:T(8,128)(2,1)} async-done(((bf16[1,16,2,4,16,256]{5,1,2,4,0,3:T(8,128)(2,1)}), bf16[1,16,2,4,16,256]{5,1,2,4,0,3:T(8,128)(2,1)}, u32[]{:S(2)}, u32[]{:S(2)}) %all-to-all-start.2) | async-done | bytes 1048608 | tf_op jit(solution)/shard_map/all_to_all | solution.py:17
  165.6 4.2 %all-to-all-start.7 = ((bf16[1,16,2,4,16,256]{5,1,2,4,0,3:T(8,128)(2,1)}), bf16[1,16,2,4,16,256]{5,1,2,4,0,3:T(8,128)(2,1)}, u32[]{:S(2)}, u32[]{:S(2)}) async-start(bf16[1,16,2,4,16,256]{5,1,2,4,0,3:T(8,128)(2,1)} %bitcast.136), calls=%async_computation.7 | async-start | bytes 2097152 | tf_op jit(solution)/shard_map/all_to_all | solution.py:17
  170.1 3.6 %fusion.15 = f32[16,128,128]{2,1,0:T(8,128)} fusion(bf16[16,128,256]{2,1,0:T(8,128)(2,1)} %bitcast.150, f32[16,128,256]{2,1,0:T(8,128)} %bitcast.148), kind=kOutput, calls=%fused_computation.45 | convolution fusion | flops 138936320 | bytes 4194304 | tf_op jit(solution)/shard_map/nct,ndt->ncd/dot_general | solution.py:30
  173.7 2.4 stack.27
  176.1 2.6 fusion.16
  178.8 2.4 stack.26
  181.2 1.8 copy.63
  184.4 1.3 stack.28
  185.7 1.8 copy.74
  187.5 1.5 convolution_bitcast_fusion
  189.0 1.6 copy.75
  190.6 1.4 stack.25
  192.0 5.4 %fusion.2 = f32[4,16,16384]{2,1,0:T(8,128)} fusion(bf16[1,4,16,16384]{3,2,1,0:T(8,128)(2,1)} %param.9, f32[1,16,16384]{2,1,0:T(8,128)} %stack.28, f32[1,16,16384]{2,1,0:T(8,128)} %stack.27, f32[1,16,16384]{2,1,0:T(8,128)} %stack.26, f32[1,16,16384]{2,1,0:T(8,128)} %stack.25, f32[4,16]{1,0:T(4,128)S(1)} %shift-left_convert_fusion), kind=kLoop, calls=%fused_computation.4 | loop fusion | flops 7340032 | bytes 10486016 | tf_op jit(solution)/shard_map/jit(clip)/min | solution.py:38
  197.4 1.2 copy-done.4
  198.6 1.5 convolution_convert_fusion.2
  201.2 4.4 %all-to-all-start.3 = ((bf16[1,16,2,4,16,256]{5,1,2,4,0,3:T(8,128)(2,1)}), bf16[1,16,2,4,16,256]{5,1,2,4,0,3:T(8,128)(2,1)}, u32[]{:S(2)}, u32[]{:S(2)}) async-start(bf16[1,16,2,4,16,256]{5,1,2,4,0,3:T(8,128)(2,1)} %bitcast.139), calls=%async_computation.3 | async-start | bytes 2097152 | tf_op jit(solution)/shard_map/all_to_all | solution.py:17
  205.6 2.4 stack.32
  208.0 1.2 stack.31
  209.2 2.5 stack.33
  211.7 1.2 stack.30
  212.8 7.2 %all-to-all-done.3 = bf16[1,16,2,4,16,256]{5,1,2,4,0,3:T(8,128)(2,1)} async-done(((bf16[1,16,2,4,16,256]{5,1,2,4,0,3:T(8,128)(2,1)}), bf16[1,16,2,4,16,256]{5,1,2,4,0,3:T(8,128)(2,1)}, u32[]{:S(2)}, u32[]{:S(2)}) %all-to-all-start.3) | async-done | bytes 1048608 | tf_op jit(solution)/shard_map/all_to_all | solution.py:17
  220.1 1.9 copy.66
  222.1 1.4 fusion.10
  223.5 1.3 fusion.11
  225.9 1.9 subtract_convert_fusion
  227.9 56.8 %reduce-scatter.2.cloned.1.call-done = f32[4,16,2048]{2,1,0:T(8,128)} async-done(((f32[4,16,16384]{2,1,0:T(8,128)}), f32[4,16,2048]{2,1,0:T(8,128)}) %reduce-scatter.2.cloned.1.call-update) | async-done | bytes 524304 | tf_op jit(solution)/shard_map/reduce_scatter | solution.py:77
  284.7 1.9 divide_multiply_fusion
  (71 shorter events, 15.9 us)
Async XLA Ops:
  7.2 54.8 %all-gather.2.cloned.1.call-start = ((), (), s32[]{:S(2)}) async-start(), calls=%async_computation.9 | async-start | bytes 2359296 | tf_op jit(solution)/shard_map/all_gather | solution.py:46
  10.7 56.5 %all-to-all-start.4 = ((bf16[1,16,2,4,16,256]{5,4,2,1,0,3:T(8,128)(2,1)}), bf16[1,16,2,4,16,256]{5,4,2,1,0,3:T(8,128)(2,1)S(1)}, u32[]{:S(2)}, u32[]{:S(2)}) async-start(bf16[1,16,2,4,16,256]{5,4,2,1,0,3:T(8,128)(2,1)} %copy.67), calls=%async_computation.4 | async-start | bytes 2097152 | tf_op jit(solution)/shard_map/all_to_all | solution.py:17
  14.9 50.6 %copy-start = (bf16[2048,256]{1,0:T(8,128)(2,1)S(1)}, bf16[2048,256]{1,0:T(8,128)(2,1)}, u32[]{:S(2)}) copy-start(bf16[2048,256]{1,0:T(8,128)(2,1)} %param.5) | copy-start | bytes 3145732
  64.8 0.8 copy-start.9
  67.2 18.7 %all-to-all-start = ((bf16[1,16,2,4,16,256]{5,1,2,4,0,3:T(8,128)(2,1)}), bf16[1,16,2,4,16,256]{5,1,2,4,0,3:T(8,128)(2,1)}, u32[]{:S(2)}, u32[]{:S(2)}) async-start(bf16[1,16,2,4,16,256]{5,1,2,4,0,3:T(8,128)(2,1)} %bitcast.115), calls=%async_computation | async-start | bytes 2097152 | tf_op jit(solution)/shard_map/all_to_all | solution.py:17
  71.4 1.0 copy-start.21
  72.6 0.8 copy-start.11
  73.8 16.4 %copy-start.20 = (bf16[2,8,128,128]{3,1,2,0:T(8,128)(2,1)S(1)}, bf16[2,8,128,128]{3,1,2,0:T(8,128)(2,1)}, u32[]{:S(2)}) copy-start(bf16[2,8,128,128]{3,1,2,0:T(8,128)(2,1)} %get-tuple-element.6) | copy-start | bytes 1572868
  85.9 18.7 %all-to-all-start.5 = ((bf16[1,16,2,4,16,256]{5,1,2,4,0,3:T(8,128)(2,1)}), bf16[1,16,2,4,16,256]{5,1,2,4,0,3:T(8,128)(2,1)}, u32[]{:S(2)}, u32[]{:S(2)}) async-start(bf16[1,16,2,4,16,256]{5,1,2,4,0,3:T(8,128)(2,1)} %bitcast.111), calls=%async_computation.5 | async-start | bytes 2097152 | tf_op jit(solution)/shard_map/all_to_all | solution.py:17
  90.3 2.5 copy-start.12
  104.7 18.7 %all-to-all-start.1 = ((bf16[1,16,2,4,16,256]{5,1,2,4,0,3:T(8,128)(2,1)}), bf16[1,16,2,4,16,256]{5,1,2,4,0,3:T(8,128)(2,1)}, u32[]{:S(2)}, u32[]{:S(2)}) async-start(bf16[1,16,2,4,16,256]{5,1,2,4,0,3:T(8,128)(2,1)} %bitcast.138), calls=%async_computation.1 | async-start | bytes 2097152 | tf_op jit(solution)/shard_map/all_to_all | solution.py:17
  123.4 2.0 copy-start.22
  123.4 2.0 copy-start.23
  125.4 1.6 copy-start.19
  128.1 18.7 %all-to-all-start.6 = ((bf16[1,16,2,4,16,256]{5,1,2,4,0,3:T(8,128)(2,1)}), bf16[1,16,2,4,16,256]{5,1,2,4,0,3:T(8,128)(2,1)}, u32[]{:S(2)}, u32[]{:S(2)}) async-start(bf16[1,16,2,4,16,256]{5,1,2,4,0,3:T(8,128)(2,1)} %bitcast.140), calls=%async_computation.6 | async-start | bytes 2097152 | tf_op jit(solution)/shard_map/all_to_all | solution.py:17
  135.0 16.2 %copy-start.24 = (s32[4,16]{1,0:T(4,128)S(1)}, s32[4,16]{1,0:T(4,128)}, u32[]{:S(2)}) copy-start(s32[4,16]{1,0:T(4,128)} %param.8) | copy-start | bytes 772
  146.8 18.7 %all-to-all-start.2 = ((bf16[1,16,2,4,16,256]{5,1,2,4,0,3:T(8,128)(2,1)}), bf16[1,16,2,4,16,256]{5,1,2,4,0,3:T(8,128)(2,1)}, u32[]{:S(2)}, u32[]{:S(2)}) async-start(bf16[1,16,2,4,16,256]{5,1,2,4,0,3:T(8,128)(2,1)} %bitcast.137), calls=%async_computation.2 | async-start | bytes 2097152 | tf_op jit(solution)/shard_map/all_to_all | solution.py:17
  151.1 2.9 copy-start.13
  153.0 1.0 copy-start.5
  165.6 20.1 %all-to-all-start.7 = ((bf16[1,16,2,4,16,256]{5,1,2,4,0,3:T(8,128)(2,1)}), bf16[1,16,2,4,16,256]{5,1,2,4,0,3:T(8,128)(2,1)}, u32[]{:S(2)}, u32[]{:S(2)}) async-start(bf16[1,16,2,4,16,256]{5,1,2,4,0,3:T(8,128)(2,1)} %bitcast.136), calls=%async_computation.7 | async-start | bytes 2097152 | tf_op jit(solution)/shard_map/all_to_all | solution.py:17
  169.9 114.8 %reduce-scatter.2.cloned.1.call-start = ((), (), s32[]{:S(2)}) async-start(), calls=%async_computation.10 | async-start | bytes 4718592 | tf_op jit(solution)/shard_map/reduce_scatter | solution.py:77
  183.0 1.0 copy-start.3
  184.4 3.1 %copy-start.2 = (f32[16,128,128]{2,1,0:T(8,128)}, f32[16,128,128]{2,1,0:T(8,128)S(1)}, u32[]{:S(2)}) copy-start(f32[16,128,128]{2,1,0:T(8,128)S(1)} %fusion.17) | copy-start | bytes 3145732
  190.6 6.8 %copy-start.6 = (f32[16,128,128]{2,1,0:T(8,128)}, f32[16,128,128]{2,1,0:T(8,128)S(1)}, u32[]{:S(2)}) copy-start(f32[16,128,128]{2,1,0:T(8,128)S(1)} %copy.75) | copy-start | bytes 3145732
  197.3 1.2 copy-start.4
  201.2 6.8 %copy-start.1 = (f32[16,128,128]{2,1,0:T(8,128)S(1)}, f32[16,128,128]{2,1,0:T(8,128)}, u32[]{:S(2)}) copy-start(f32[16,128,128]{2,1,0:T(8,128)} %fusion.16) | copy-start | bytes 3145732
  201.2 18.9 %all-to-all-start.3 = ((bf16[1,16,2,4,16,256]{5,1,2,4,0,3:T(8,128)(2,1)}), bf16[1,16,2,4,16,256]{5,1,2,4,0,3:T(8,128)(2,1)}, u32[]{:S(2)}, u32[]{:S(2)}) async-start(bf16[1,16,2,4,16,256]{5,1,2,4,0,3:T(8,128)(2,1)} %bitcast.139), calls=%async_computation.3 | async-start | bytes 2097152 | tf_op jit(solution)/shard_map/all_to_all | solution.py:17
  209.2 2.5 copy-start.7
  212.8 9.2 %copy-start.10 = (bf16[2,8,128,128]{3,2,1,0:T(8,128)(2,1)S(1)}, bf16[2,8,128,128]{3,2,1,0:T(8,128)(2,1)}, u32[]{:S(2)}) copy-start(bf16[2,8,128,128]{3,2,1,0:T(8,128)(2,1)} %copy-done.9) | copy-start | bytes 1572868
  220.1 1.9 copy-start.14
  222.0 2.7 copy-start.16
  222.0 2.7 copy-start.17
  222.0 2.7 copy-start.18
  223.5 2.2 copy-start.8
  223.5 2.5 copy-start.15
Sparse Core Ops, SparseCore 0:
  10.2 51.7 all-gather.1
  197.5 87.1 reduce-scatter.1
where the time goes:
time: 295 us; the launch traced here: 293 us
  waiting for transfers between devices  164 us (56%)
  local copies, waits for them, and re-layouts  52.9 us (18%)
  starting transfers between devices  34.4 us (12%)
  matrix products  17.1 us (6%)
  between operations  14.4 us (5%)
  other arithmetic  10.6 us (4%)
    all_to_all x8, waiting for transfers between devices, regroup(): lax.all_to_all(shaped, 'ma', split_axis=3, concat_axis=3, tiled=True)  59.6 us
    reduce_scatter x1, waiting for transfers between devices, body(): lax.psum_scatter(code_values, 'dev', scatter_dimension=2, tiled=True)  56.8 us
    all_gather x1, waiting for transfers between devices, body(): gathered = lax.all_gather(factors, 'dev', axis=2, tiled=True)  47 us
    all_to_all x8, starting transfers between devices, regroup(): lax.all_to_all(shaped, 'ma', split_axis=3, concat_axis=3, tiled=True)  34.1 us
    another operation x8, local copies, waits for them, and re-layouts, body(): jnp.stack([gradient_zero, gradient_one, gradient_two, gradient_three])  14.7 us
    all_to_all x7, local copies, waits for them, and re-layouts, regroup(): lax.all_to_all(shaped, 'ma', split_axis=3, concat_axis=3, tiled=True)  12.3 us
    unnamed x55, local copies, waits for them, and re-layouts  11.8 us
    dot_general x4, matrix products, outer_sum(): jnp.einsum('nct,ndt->ncd', left, right, preferred_element_type=jnp.float32)  8.22 us
  transfers between devices with their start and end apart: 10, of which 8 were waited for; matrix products, arithmetic and copies ran while one was open for 19% of the time, Pallas kernels for 0%

commit v1 on v0

--- a/solution.py
+++ b/solution.py
@@ -5,6 +5,17 @@
 
 B = 128
 code_limit = 127.0
+
+
+def gather_around(shard, axis, dim):
+    ways = lax.axis_size(axis)
+    pieces = [shard]
+    for far in range(1, ways):
+        pieces.append(
+            lax.ppermute(pieces[far - 1], axis, [(d, (d - 1) % ways) for d in range(ways)])
+        )
+    line = jnp.concatenate(pieces, axis=dim)
+    return jnp.roll(line, lax.axis_index(axis) * shard.shape[dim], axis=dim)
 
 
 def regroup(stacked):
@@ -43,7 +54,7 @@
     local_blocks = factors.shape[1]
     tok_count = inputs.shape[1]
     group_count = lax.axis_size("dev")
-    gathered = lax.all_gather(factors, "dev", axis=2, tiled=True)
+    gathered = gather_around(factors, "dev", 2)
     matrices = gathered.reshape(gathered.shape[0], local_blocks, B, B)
     block_in = inputs.reshape(local_blocks, B, tok_count)
     block_cot = cotangent.reshape(local_blocks, B, tok_count)

time: 295 us -> 311 us (1.054)
  starting transfers between devices: 34.4 us -> 65.1 us
  waiting for transfers between devices: 164 us -> 147 us
  matrix products: 17.1 us -> 22.2 us
    all_gather x1 -> x0, waiting for transfers between devices: 47 us -> none  [body(): gathered = lax.all_gather(factors, 'dev', axis=2, tiled=True)]
    ppermute x0 -> x7, starting transfers between devices: none -> 31.6 us  [gather_around(): lax.ppermute(pieces[far - 1], axis, [(d, (d - 1) % ways) for d in range(w...]
    ppermute x0 -> x7, waiting for transfers between devices: none -> 29 us  [gather_around(): lax.ppermute(pieces[far - 1], axis, [(d, (d - 1) % ways) for d in range(w...]
    dot_general x4, matrix products: 3.79 us -> 8.47 us  [block_backward(): jnp.einsum('ncd,ndt->nct', weights, values, preferred_element_type=jnp.fl...]
    reduce_scatter x1, waiting for transfers between devices: 56.8 us -> 60.6 us  [body(): lax.psum_scatter(code_values, 'dev', scatter_dimension=2, tiled=True)]
    unnamed x55 -> x58, local copies, waits for them, and re-layouts: 11.8 us -> 8.34 us
  transfers between devices with their start and end apart: 10 -> 16, of which waited for: 8 -> 13; matrix products, arithmetic and copies ran while one was open for 19% -> 19% of each run, Pallas kernels for 0% -> 0%
where the time goes in v1:
time: 311 us; the launch traced here: 310 us
  waiting for transfers between devices  147 us (47%)
  starting transfers between devices  65.1 us (21%)
  local copies, waits for them, and re-layouts  50.6 us (16%)
  matrix products  22.2 us (7%)
  between operations  14.5 us (5%)
  other arithmetic  10.6 us (3%)
    reduce_scatter x1, waiting for transfers between devices, body(): lax.psum_scatter(code_values, 'dev', scatter_dimension=2, tiled=True)  60.6 us
    all_to_all x8, waiting for transfers between devices, regroup(): lax.all_to_all(shaped, 'ma', split_axis=3, concat_axis=3, tiled=True)  57.1 us
    all_to_all x8, starting transfers between devices, regroup(): lax.all_to_all(shaped, 'ma', split_axis=3, concat_axis=3, tiled=True)  33.3 us
    ppermute x7, starting transfers between devices, gather_around(): lax.ppermute(pieces[far - 1], axis, [(d, (d - 1) % ways) for d in range(w...  31.6 us
    ppermute x7, waiting for transfers between devices, gather_around(): lax.ppermute(pieces[far - 1], axis, [(d, (d - 1) % ways) for d in range(w...  29 us
    another operation x8, local copies, waits for them, and re-layouts, body(): jnp.stack([gradient_zero, gradient_one, gradient_two, gradient_three])  16 us
    all_to_all x7, local copies, waits for them, and re-layouts, regroup(): lax.all_to_all(shaped, 'ma', split_axis=3, concat_axis=3, tiled=True)  12.3 us
    dot_general x4, matrix products, block_backward(): jnp.einsum('ncd,ndt->nct', weights, values, preferred_element_type=jnp.fl...  8.47 us
  transfers between devices with their start and end apart: 16, of which 13 were waited for; matrix products, arithmetic and copies ran while one was open for 19% of the time, Pallas kernels for 0%

profile of v1, /device:TPU:0, one launch (start us, length us, event | category | flops | bytes accessed | tf_op | source)
XLA Modules:
  0.0 309.7 jit_solution(13776655871233459892)
XLA Ops:
  7.2 6.1 %collective-permute-start = (bf16[4,16,2048]{2,1,0:T(8,128)(2,1)}, bf16[4,16,2048]{2,1,0:T(8,128)(2,1)S(1)}, u32[]{:S(2)}, u32[]{:S(2)}) collective-permute-start(bf16[4,16,2048]{2,1,0:T(8,128)(2,1)} %param.7), channel_id=1, source_target_pairs={{0,28},{4,0},{8,4},{12,8},{16,12},{20,16},{24,20},{28,24},{1,29},{... | collective-permute-start | bytes 786440 | tf_op jit(solution)/shard_map/ppermute | solution.py:15
  13.2 5.9 %collective-permute-done = bf16[4,16,2048]{2,1,0:T(8,128)(2,1)S(1)} collective-permute-done((bf16[4,16,2048]{2,1,0:T(8,128)(2,1)}, bf16[4,16,2048]{2,1,0:T(8,128)(2,1)S(1)}, u32[]{:S(2)}, u32[]{:S(2)}) %collective-permute-start) | collective-permute-done | bytes 262176 | tf_op jit(solution)/shard_map/ppermute | solution.py:15
  19.1 5.1 %collective-permute-start.1 = (bf16[4,16,2048]{2,1,0:T(8,128)(2,1)S(1)}, bf16[4,16,2048]{2,1,0:T(8,128)(2,1)S(1)}, u32[]{:S(2)}, u32[]{:S(2)}) collective-permute-start(bf16[4,16,2048]{2,1,0:T(8,128)(2,1)S(1)} %collective-permute-done), channel_id=1, source_target_pairs={{0,28},{4,0},{8,4},{12,8},{16,12},{20,16},{24,20},{28,24},{1,29},{... | collective-permute-start | bytes 786440 | tf_op jit(solution)/shard_map/ppermute | solution.py:15
  24.2 4.7 %collective-permute-done.1 = bf16[4,16,2048]{2,1,0:T(8,128)(2,1)S(1)} collective-permute-done((bf16[4,16,2048]{2,1,0:T(8,128)(2,1)S(1)}, bf16[4,16,2048]{2,1,0:T(8,128)(2,1)S(1)}, u32[]{:S(2)}, u32[]{:S(2)}) %collective-permute-start.1) | collective-permute-done | bytes 262176 | tf_op jit(solution)/shard_map/ppermute | solution.py:15
  28.9 5.2 %collective-permute-start.2 = (bf16[4,16,2048]{2,1,0:T(8,128)(2,1)S(1)}, bf16[4,16,2048]{2,1,0:T(8,128)(2,1)S(1)}, u32[]{:S(2)}, u32[]{:S(2)}) collective-permute-start(bf16[4,16,2048]{2,1,0:T(8,128)(2,1)S(1)} %collective-permute-done.1), channel_id=1, source_target_pairs={{0,28},{4,0},{8,4},{12,8},{16,12},{20,16},{24,20},{28,24},{1,29},{... | collective-permute-start | bytes 786440 | tf_op jit(solution)/shard_map/ppermute | solution.py:15
  34.1 3.9 %collective-permute-done.2 = bf16[4,16,2048]{2,1,0:T(8,128)(2,1)S(1)} collective-permute-done((bf16[4,16,2048]{2,1,0:T(8,128)(2,1)S(1)}, bf16[4,16,2048]{2,1,0:T(8,128)(2,1)S(1)}, u32[]{:S(2)}, u32[]{:S(2)}) %collective-permute-start.2) | collective-permute-done | bytes 262176 | tf_op jit(solution)/shard_map/ppermute | solution.py:15
  38.0 5.2 %collective-permute-start.3 = (bf16[4,16,2048]{2,1,0:T(8,128)(2,1)S(1)}, bf16[4,16,2048]{2,1,0:T(8,128)(2,1)S(1)}, u32[]{:S(2)}, u32[]{:S(2)}) collective-permute-start(bf16[4,16,2048]{2,1,0:T(8,128)(2,1)S(1)} %collective-permute-done.2), channel_id=1, source_target_pairs={{0,28},{4,0},{8,4},{12,8},{16,12},{20,16},{24,20},{28,24},{1,29},{... | collective-permute-start | bytes 786440 | tf_op jit(solution)/shard_map/ppermute | solution.py:15
  43.1 2.8 copy.67
  45.9 3.5 %all-to-all-start.4 = ((bf16[1,16,2,4,16,256]{5,4,2,1,0,3:T(8,128)(2,1)}), bf16[1,16,2,4,16,256]{5,4,2,1,0,3:T(8,128)(2,1)S(1)}, u32[]{:S(2)}, u32[]{:S(2)}) async-start(bf16[1,16,2,4,16,256]{5,4,2,1,0,3:T(8,128)(2,1)} %copy.67), calls=%async_computation.4 | async-start | bytes 2097152 | tf_op jit(solution)/shard_map/all_to_all | solution.py:28
  49.5 2.7 collective-permute-start.4
  52.3 6.0 %collective-permute-done.4 = bf16[4,16,2048]{2,1,0:T(8,128)(2,1)S(1)} collective-permute-done((bf16[4,16,2048]{2,1,0:T(8,128)(2,1)S(1)}, bf16[4,16,2048]{2,1,0:T(8,128)(2,1)S(1)}, u32[]{:S(2)}, u32[]{:S(2)}) %collective-permute-start.4) | collective-permute-done | bytes 262176 | tf_op jit(solution)/shard_map/ppermute | solution.py:15
  58.2 3.1 collective-permute-start.5
  61.3 4.7 %collective-permute-done.5 = bf16[4,16,2048]{2,1,0:T(8,128)(2,1)S(1)} collective-permute-done((bf16[4,16,2048]{2,1,0:T(8,128)(2,1)S(1)}, bf16[4,16,2048]{2,1,0:T(8,128)(2,1)S(1)}, u32[]{:S(2)}, u32[]{:S(2)}) %collective-permute-start.5) | collective-permute-done | bytes 262176 | tf_op jit(solution)/shard_map/ppermute | solution.py:15
  66.0 4.3 %collective-permute-start.6 = (bf16[4,16,2048]{2,1,0:T(8,128)(2,1)S(1)}, bf16[4,16,2048]{2,1,0:T(8,128)(2,1)S(1)}, u32[]{:S(2)}, u32[]{:S(2)}) collective-permute-start(bf16[4,16,2048]{2,1,0:T(8,128)(2,1)S(1)} %collective-permute-done.5), channel_id=1, source_target_pairs={{0,28},{4,0},{8,4},{12,8},{16,12},{20,16},{24,20},{28,24},{1,29},{... | collective-permute-start | bytes 786440 | tf_op jit(solution)/shard_map/ppermute | solution.py:15
  70.4 3.8 %collective-permute-done.6 = bf16[4,16,2048]{2,1,0:T(8,128)(2,1)S(1)} collective-permute-done((bf16[4,16,2048]{2,1,0:T(8,128)(2,1)S(1)}, bf16[4,16,2048]{2,1,0:T(8,128)(2,1)S(1)}, u32[]{:S(2)}, u32[]{:S(2)}) %collective-permute-start.6) | collective-permute-done | bytes 262176 | tf_op jit(solution)/shard_map/ppermute | solution.py:15
  78.2 4.2 %all-to-all-start = ((bf16[1,16,2,4,16,256]{5,1,2,4,0,3:T(8,128)(2,1)}), bf16[1,16,2,4,16,256]{5,1,2,4,0,3:T(8,128)(2,1)}, u32[]{:S(2)}, u32[]{:S(2)}) async-start(bf16[1,16,2,4,16,256]{5,1,2,4,0,3:T(8,128)(2,1)} %bitcast.92), calls=%async_computation | async-start | bytes 2097152 | tf_op jit(solution)/shard_map/all_to_all | solution.py:28
  86.1 10.8 %all-to-all-done = bf16[1,16,2,4,16,256]{5,1,2,4,0,3:T(8,128)(2,1)} async-done(((bf16[1,16,2,4,16,256]{5,1,2,4,0,3:T(8,128)(2,1)}), bf16[1,16,2,4,16,256]{5,1,2,4,0,3:T(8,128)(2,1)}, u32[]{:S(2)}, u32[]{:S(2)}) %all-to-all-start) | async-done | bytes 1048608 | tf_op jit(solution)/shard_map/all_to_all | solution.py:28
  96.9 4.2 %all-to-all-start.5 = ((bf16[1,16,2,4,16,256]{5,1,2,4,0,3:T(8,128)(2,1)}), bf16[1,16,2,4,16,256]{5,1,2,4,0,3:T(8,128)(2,1)}, u32[]{:S(2)}, u32[]{:S(2)}) async-start(bf16[1,16,2,4,16,256]{5,1,2,4,0,3:T(8,128)(2,1)} %bitcast.88), calls=%async_computation.5 | async-start | bytes 2097152 | tf_op jit(solution)/shard_map/all_to_all | solution.py:28
  101.3 2.0 copy.57
  104.9 10.8 %all-to-all-done.5 = bf16[1,16,2,4,16,256]{5,1,2,4,0,3:T(8,128)(2,1)} async-done(((bf16[1,16,2,4,16,256]{5,1,2,4,0,3:T(8,128)(2,1)}), bf16[1,16,2,4,16,256]{5,1,2,4,0,3:T(8,128)(2,1)}, u32[]{:S(2)}, u32[]{:S(2)}) %all-to-all-start.5) | async-done | bytes 1048608 | tf_op jit(solution)/shard_map/all_to_all | solution.py:28
  115.7 4.2 %all-to-all-start.1 = ((bf16[1,16,2,4,16,256]{5,1,2,4,0,3:T(8,128)(2,1)}), bf16[1,16,2,4,16,256]{5,1,2,4,0,3:T(8,128)(2,1)}, u32[]{:S(2)}, u32[]{:S(2)}) async-start(bf16[1,16,2,4,16,256]{5,1,2,4,0,3:T(8,128)(2,1)} %bitcast.115), calls=%async_computation.1 | async-start | bytes 2097152 | tf_op jit(solution)/shard_map/all_to_all | solution.py:28
  119.9 1.9 copy.82
  121.8 2.8 copy.70
  124.6 9.8 %all-to-all-done.1 = bf16[1,16,2,4,16,256]{5,1,2,4,0,3:T(8,128)(2,1)} async-done(((bf16[1,16,2,4,16,256]{5,1,2,4,0,3:T(8,128)(2,1)}), bf16[1,16,2,4,16,256]{5,1,2,4,0,3:T(8,128)(2,1)}, u32[]{:S(2)}, u32[]{:S(2)}) %all-to-all-start.1) | async-done | bytes 1048608 | tf_op jit(solution)/shard_map/all_to_all | solution.py:28
  134.4 1.8 copy.60
  136.3 3.7 %fusion.9 = bf16[16,128,256]{2,1,0:T(8,128)(2,1)S(1)} fusion(f32[16,128,256]{2,1,0:T(8,128)S(1)} %bitcast.123, bf16[16,128,128]{2,1,0:T(8,128)(2,1)} %bitcast.131, bf16[16,128,256]{2,1,0:T(8,128)(2,1)} %bitcast.127), kind=kOutput, calls=%fused_computation.14 | convolution fusion | flops 144703488 | bytes 4718592 | tf_op jit(solution)/shard_map/ncd,ndt->nct/dot_general | solution.py:37
  141.1 4.2 %all-to-all-start.6 = ((bf16[1,16,2,4,16,256]{5,1,2,4,0,3:T(8,128)(2,1)}), bf16[1,16,2,4,16,256]{5,1,2,4,0,3:T(8,128)(2,1)}, u32[]{:S(2)}, u32[]{:S(2)}) async-start(bf16[1,16,2,4,16,256]{5,1,2,4,0,3:T(8,128)(2,1)} %bitcast.117), calls=%async_computation.6 | async-start | bytes 2097152 | tf_op jit(solution)/shard_map/all_to_all | solution.py:28
  145.3 2.7 convolution_convert_fusion.3
  149.1 10.7 %all-to-all-done.6 = bf16[1,16,2,4,16,256]{5,1,2,4,0,3:T(8,128)(2,1)} async-done(((bf16[1,16,2,4,16,256]{5,1,2,4,0,3:T(8,128)(2,1)}), bf16[1,16,2,4,16,256]{5,1,2,4,0,3:T(8,128)(2,1)}, u32[]{:S(2)}, u32[]{:S(2)}) %all-to-all-start.6) | async-done | bytes 1048608 | tf_op jit(solution)/shard_map/all_to_all | solution.py:28
  159.8 4.3 %all-to-all-start.2 = ((bf16[1,16,2,4,16,256]{5,1,2,4,0,3:T(8,128)(2,1)}), bf16[1,16,2,4,16,256]{5,1,2,4,0,3:T(8,128)(2,1)}, u32[]{:S(2)}, u32[]{:S(2)}) async-start(bf16[1,16,2,4,16,256]{5,1,2,4,0,3:T(8,128)(2,1)} %bitcast.114), calls=%async_computation.2 | async-start | bytes 2097152 | tf_op jit(solution)/shard_map/all_to_all | solution.py:28
  169.5 9.1 %all-to-all-done.2 = bf16[1,16,2,4,16,256]{5,1,2,4,0,3:T(8,128)(2,1)} async-done(((bf16[1,16,2,4,16,256]{5,1,2,4,0,3:T(8,128)(2,1)}), bf16[1,16,2,4,16,256]{5,1,2,4,0,3:T(8,128)(2,1)}, u32[]{:S(2)}, u32[]{:S(2)}) %all-to-all-start.2) | async-done | bytes 1048608 | tf_op jit(solution)/shard_map/all_to_all | solution.py:28
  178.6 4.2 %all-to-all-start.7 = ((bf16[1,16,2,4,16,256]{5,1,2,4,0,3:T(8,128)(2,1)}), bf16[1,16,2,4,16,256]{5,1,2,4,0,3:T(8,128)(2,1)}, u32[]{:S(2)}, u32[]{:S(2)}) async-start(bf16[1,16,2,4,16,256]{5,1,2,4,0,3:T(8,128)(2,1)} %bitcast.113), calls=%async_computation.7 | async-start | bytes 2097152 | tf_op jit(solution)/shard_map/all_to_all | solution.py:28
  183.0 3.6 %fusion.12 = f32[16,128,128]{2,1,0:T(8,128)} fusion(bf16[16,128,256]{2,1,0:T(8,128)(2,1)} %bitcast.128, f32[16,128,256]{2,1,0:T(8,128)} %bitcast.125), kind=kOutput, calls=%fused_computation.56 | convolution fusion | flops 138936320 | bytes 4194304 | tf_op jit(solution)/shard_map/nct,ndt->ncd/dot_general | solution.py:41
  186.7 2.5 stack.27
  193.4 2.4 stack.28
  198.8 1.8 copy.74
  204.9 5.4 %fusion.2 = f32[4,16,16384]{2,1,0:T(8,128)} fusion(bf16[1,4,16,16384]{3,2,1,0:T(8,128)(2,1)} %param.9, f32[1,16,16384]{2,1,0:T(8,128)} %stack.28, f32[1,16,16384]{2,1,0:T(8,128)} %stack.27, f32[1,16,16384]{2,1,0:T(8,128)} %stack.26, f32[1,16,16384]{2,1,0:T(8,128)} %stack.25, f32[4,16]{1,0:T(4,128)S(1)} %shift-left_convert_fusion), kind=kLoop, calls=%fused_computation.4 | loop fusion | flops 7340032 | bytes 10486016 | tf_op jit(solution)/shard_map/jit(clip)/min | solution.py:49
  210.3 2.0 convolution_convert_fusion.2
  213.3 4.3 %all-to-all-start.3 = ((bf16[1,16,2,4,16,256]{5,1,2,4,0,3:T(8,128)(2,1)}), bf16[1,16,2,4,16,256]{5,1,2,4,0,3:T(8,128)(2,1)}, u32[]{:S(2)}, u32[]{:S(2)}) async-start(bf16[1,16,2,4,16,256]{5,1,2,4,0,3:T(8,128)(2,1)} %bitcast.116), calls=%async_computation.3 | async-start | bytes 2097152 | tf_op jit(solution)/shard_map/all_to_all | solution.py:28
  217.6 2.5 stack.32
  221.3 2.5 stack.31
  223.7 2.4 stack.30
  226.1 6.0 %all-to-all-done.3 = bf16[1,16,2,4,16,256]{5,1,2,4,0,3:T(8,128)(2,1)} async-done(((bf16[1,16,2,4,16,256]{5,1,2,4,0,3:T(8,128)(2,1)}), bf16[1,16,2,4,16,256]{5,1,2,4,0,3:T(8,128)(2,1)}, u32[]{:S(2)}, u32[]{:S(2)}) %all-to-all-start.3) | async-done | bytes 1048608 | tf_op jit(solution)/shard_map/all_to_all | solution.py:28
  232.1 2.0 copy.66
  234.1 2.9 fusion.10
  238.3 2.0 subtract_convert_fusion
  240.3 60.6 %reduce-scatter.2.cloned.1.call-done = f32[4,16,2048]{2,1,0:T(8,128)} async-done(((f32[4,16,16384]{2,1,0:T(8,128)}), f32[4,16,2048]{2,1,0:T(8,128)}) %reduce-scatter.2.cloned.1.call-update) | async-done | bytes 524304 | tf_op jit(solution)/shard_map/reduce_scatter | solution.py:88
  300.9 1.9 divide_multiply_fusion
  (86 shorter events, 32.2 us)
Async XLA Ops:
  7.2 42.3 %copy-start.17 = (bf16[4,16,2048]{2,1,0:T(8,128)(2,1)S(1)}, bf16[4,16,2048]{2,1,0:T(8,128)(2,1)}, u32[]{:S(2)}) copy-start(bf16[4,16,2048]{2,1,0:T(8,128)(2,1)} %param.7) | copy-start | bytes 786436
  7.2 11.9 %collective-permute-start = (bf16[4,16,2048]{2,1,0:T(8,128)(2,1)}, bf16[4,16,2048]{2,1,0:T(8,128)(2,1)S(1)}, u32[]{:S(2)}, u32[]{:S(2)}) collective-permute-start(bf16[4,16,2048]{2,1,0:T(8,128)(2,1)} %param.7), channel_id=1, source_target_pairs={{0,28},{4,0},{8,4},{12,8},{16,12},{20,16},{24,20},{28,24},{1,29},{... | collective-permute-start | bytes 786440 | tf_op jit(solution)/shard_map/ppermute | solution.py:15
  19.1 9.8 %collective-permute-start.1 = (bf16[4,16,2048]{2,1,0:T(8,128)(2,1)S(1)}, bf16[4,16,2048]{2,1,0:T(8,128)(2,1)S(1)}, u32[]{:S(2)}, u32[]{:S(2)}) collective-permute-start(bf16[4,16,2048]{2,1,0:T(8,128)(2,1)S(1)} %collective-permute-done), channel_id=1, source_target_pairs={{0,28},{4,0},{8,4},{12,8},{16,12},{20,16},{24,20},{28,24},{1,29},{... | collective-permute-start | bytes 786440 | tf_op jit(solution)/shard_map/ppermute | solution.py:15
  28.9 9.1 %collective-permute-start.2 = (bf16[4,16,2048]{2,1,0:T(8,128)(2,1)S(1)}, bf16[4,16,2048]{2,1,0:T(8,128)(2,1)S(1)}, u32[]{:S(2)}, u32[]{:S(2)}) collective-permute-start(bf16[4,16,2048]{2,1,0:T(8,128)(2,1)S(1)} %collective-permute-done.1), channel_id=1, source_target_pairs={{0,28},{4,0},{8,4},{12,8},{16,12},{20,16},{24,20},{28,24},{1,29},{... | collective-permute-start | bytes 786440 | tf_op jit(solution)/shard_map/ppermute | solution.py:15
  38.0 11.5 %collective-permute-start.3 = (bf16[4,16,2048]{2,1,0:T(8,128)(2,1)S(1)}, bf16[4,16,2048]{2,1,0:T(8,128)(2,1)S(1)}, u32[]{:S(2)}, u32[]{:S(2)}) collective-permute-start(bf16[4,16,2048]{2,1,0:T(8,128)(2,1)S(1)} %collective-permute-done.2), channel_id=1, source_target_pairs={{0,28},{4,0},{8,4},{12,8},{16,12},{20,16},{24,20},{28,24},{1,29},{... | collective-permute-start | bytes 786440 | tf_op jit(solution)/shard_map/ppermute | solution.py:15
  45.9 32.2 %all-to-all-start.4 = ((bf16[1,16,2,4,16,256]{5,4,2,1,0,3:T(8,128)(2,1)}), bf16[1,16,2,4,16,256]{5,4,2,1,0,3:T(8,128)(2,1)S(1)}, u32[]{:S(2)}, u32[]{:S(2)}) async-start(bf16[1,16,2,4,16,256]{5,4,2,1,0,3:T(8,128)(2,1)} %copy.67), calls=%async_computation.4 | async-start | bytes 2097152 | tf_op jit(solution)/shard_map/all_to_all | solution.py:28
  49.5 8.7 %collective-permute-start.4 = (bf16[4,16,2048]{2,1,0:T(8,128)(2,1)S(1)}, bf16[4,16,2048]{2,1,0:T(8,128)(2,1)S(1)}, u32[]{:S(2)}, u32[]{:S(2)}) collective-permute-start(bf16[4,16,2048]{2,1,0:T(8,128)(2,1)S(1)} %collective-permute-done.3), channel_id=1, source_target_pairs={{0,28},{4,0},{8,4},{12,8},{16,12},{20,16},{24,20},{28,24},{1,29},{... | collective-permute-start | bytes 786440 | tf_op jit(solution)/shard_map/ppermute | solution.py:15
  58.2 7.8 %collective-permute-start.5 = (bf16[4,16,2048]{2,1,0:T(8,128)(2,1)S(1)}, bf16[4,16,2048]{2,1,0:T(8,128)(2,1)S(1)}, u32[]{:S(2)}, u32[]{:S(2)}) collective-permute-start(bf16[4,16,2048]{2,1,0:T(8,128)(2,1)S(1)} %collective-permute-done.4), channel_id=1, source_target_pairs={{0,28},{4,0},{8,4},{12,8},{16,12},{20,16},{24,20},{28,24},{1,29},{... | collective-permute-start | bytes 786440 | tf_op jit(solution)/shard_map/ppermute | solution.py:15
  66.0 8.2 %collective-permute-start.6 = (bf16[4,16,2048]{2,1,0:T(8,128)(2,1)S(1)}, bf16[4,16,2048]{2,1,0:T(8,128)(2,1)S(1)}, u32[]{:S(2)}, u32[]{:S(2)}) collective-permute-start(bf16[4,16,2048]{2,1,0:T(8,128)(2,1)S(1)} %collective-permute-done.5), channel_id=1, source_target_pairs={{0,28},{4,0},{8,4},{12,8},{16,12},{20,16},{24,20},{28,24},{1,29},{... | collective-permute-start | bytes 786440 | tf_op jit(solution)/shard_map/ppermute | solution.py:15
  74.3 2.2 copy-start
  75.8 0.8 copy-start.7
  78.2 18.7 %all-to-all-start = ((bf16[1,16,2,4,16,256]{5,1,2,4,0,3:T(8,128)(2,1)}), bf16[1,16,2,4,16,256]{5,1,2,4,0,3:T(8,128)(2,1)}, u32[]{:S(2)}, u32[]{:S(2)}) async-start(bf16[1,16,2,4,16,256]{5,1,2,4,0,3:T(8,128)(2,1)} %bitcast.92), calls=%async_computation | async-start | bytes 2097152 | tf_op jit(solution)/shard_map/all_to_all | solution.py:28
  82.6 18.6 %copy-start.16 = (bf16[2,8,128,128]{3,1,2,0:T(8,128)(2,1)S(1)}, bf16[2,8,128,128]{3,1,2,0:T(8,128)(2,1)}, u32[]{:S(2)}) copy-start(bf16[2,8,128,128]{3,1,2,0:T(8,128)(2,1)} %get-tuple-element.5) | copy-start | bytes 1572868
  83.8 0.8 copy-start.9
  96.9 18.7 %all-to-all-start.5 = ((bf16[1,16,2,4,16,256]{5,1,2,4,0,3:T(8,128)(2,1)}), bf16[1,16,2,4,16,256]{5,1,2,4,0,3:T(8,128)(2,1)}, u32[]{:S(2)}, u32[]{:S(2)}) async-start(bf16[1,16,2,4,16,256]{5,1,2,4,0,3:T(8,128)(2,1)} %bitcast.88), calls=%async_computation.5 | async-start | bytes 2097152 | tf_op jit(solution)/shard_map/all_to_all | solution.py:28
  101.3 2.0 copy-start.10
  115.7 18.7 %all-to-all-start.1 = ((bf16[1,16,2,4,16,256]{5,1,2,4,0,3:T(8,128)(2,1)}), bf16[1,16,2,4,16,256]{5,1,2,4,0,3:T(8,128)(2,1)}, u32[]{:S(2)}, u32[]{:S(2)}) async-start(bf16[1,16,2,4,16,256]{5,1,2,4,0,3:T(8,128)(2,1)} %bitcast.115), calls=%async_computation.1 | async-start | bytes 2097152 | tf_op jit(solution)/shard_map/all_to_all | solution.py:28
  136.2 3.7 %copy-start.15 = (f32[1,16,2,4,16,256]{5,4,3,2,1,0:T(8,128)}, f32[1,16,2,4,16,256]{5,4,3,2,1,0:T(8,128)S(1)}, u32[]{:S(2)}) copy-start(f32[1,16,2,4,16,256]{5,4,3,2,1,0:T(8,128)S(1)} %copy.60) | copy-start | bytes 6291460
  141.1 18.7 %all-to-all-start.6 = ((bf16[1,16,2,4,16,256]{5,1,2,4,0,3:T(8,128)(2,1)}), bf16[1,16,2,4,16,256]{5,1,2,4,0,3:T(8,128)(2,1)}, u32[]{:S(2)}, u32[]{:S(2)}) async-start(bf16[1,16,2,4,16,256]{5,1,2,4,0,3:T(8,128)(2,1)} %bitcast.117), calls=%async_computation.6 | async-start | bytes 2097152 | tf_op jit(solution)/shard_map/all_to_all | solution.py:28
  145.3 18.8 %copy-start.18 = (s32[4,16]{1,0:T(4,128)S(1)}, s32[4,16]{1,0:T(4,128)}, u32[]{:S(2)}) copy-start(s32[4,16]{1,0:T(4,128)} %param.8) | copy-start | bytes 772
  159.8 18.8 %all-to-all-start.2 = ((bf16[1,16,2,4,16,256]{5,1,2,4,0,3:T(8,128)(2,1)}), bf16[1,16,2,4,16,256]{5,1,2,4,0,3:T(8,128)(2,1)}, u32[]{:S(2)}, u32[]{:S(2)}) async-start(bf16[1,16,2,4,16,256]{5,1,2,4,0,3:T(8,128)(2,1)} %bitcast.114), calls=%async_computation.2 | async-start | bytes 2097152 | tf_op jit(solution)/shard_map/all_to_all | solution.py:28
  165.9 1.0 copy-start.4
  178.6 20.2 %all-to-all-start.7 = ((bf16[1,16,2,4,16,256]{5,1,2,4,0,3:T(8,128)(2,1)}), bf16[1,16,2,4,16,256]{5,1,2,4,0,3:T(8,128)(2,1)}, u32[]{:S(2)}, u32[]{:S(2)}) async-start(bf16[1,16,2,4,16,256]{5,1,2,4,0,3:T(8,128)(2,1)} %bitcast.113), calls=%async_computation.7 | async-start | bytes 2097152 | tf_op jit(solution)/shard_map/all_to_all | solution.py:28
  182.8 118.1 %reduce-scatter.2.cloned.1.call-start = ((), (), s32[]{:S(2)}) async-start(), calls=%async_computation.9 | async-start | bytes 4718592 | tf_op jit(solution)/shard_map/reduce_scatter | solution.py:88
  191.0 1.0 copy-start.3
  197.4 1.3 copy-start.2
  203.5 6.7 %copy-start.5 = (f32[16,128,128]{2,1,0:T(8,128)}, f32[16,128,128]{2,1,0:T(8,128)S(1)}, u32[]{:S(2)}) copy-start(f32[16,128,128]{2,1,0:T(8,128)S(1)} %copy.75) | copy-start | bytes 3145732
  210.3 9.8 %copy-start.1 = (f32[16,128,128]{2,1,0:T(8,128)S(1)}, f32[16,128,128]{2,1,0:T(8,128)}, u32[]{:S(2)}) copy-start(f32[16,128,128]{2,1,0:T(8,128)} %fusion.14) | copy-start | bytes 3145732
  213.3 18.8 %all-to-all-start.3 = ((bf16[1,16,2,4,16,256]{5,1,2,4,0,3:T(8,128)(2,1)}), bf16[1,16,2,4,16,256]{5,1,2,4,0,3:T(8,128)(2,1)}, u32[]{:S(2)}, u32[]{:S(2)}) async-start(bf16[1,16,2,4,16,256]{5,1,2,4,0,3:T(8,128)(2,1)} %bitcast.116), calls=%async_computation.3 | async-start | bytes 2097152 | tf_op jit(solution)/shard_map/all_to_all | solution.py:28
  221.3 12.8 %copy-start.8 = (bf16[2,8,128,128]{3,2,1,0:T(8,128)(2,1)S(1)}, bf16[2,8,128,128]{3,2,1,0:T(8,128)(2,1)}, u32[]{:S(2)}) copy-start(bf16[2,8,128,128]{3,2,1,0:T(8,128)(2,1)} %copy-done.7) | copy-start | bytes 1572868
  232.1 6.2 %copy-start.6 = (bf16[1,4,16,16384]{3,2,1,0:T(8,128)(2,1)S(1)}, bf16[1,4,16,16384]{3,2,1,0:T(8,128)(2,1)}, u32[]{:S(2)}) copy-start(bf16[1,4,16,16384]{3,2,1,0:T(8,128)(2,1)} %param.9) | copy-start | bytes 6291460
  232.1 6.2 %copy-start.11 = (f32[1,1,16,16384]{3,2,1,0:T(8,128)S(1)}, f32[1,1,16,16384]{3,2,1,0:T(8,128)}, u32[]{:S(2)}) copy-start(f32[1,1,16,16384]{3,2,1,0:T(8,128)} %stack.32) | copy-start | bytes 3145732
  232.1 6.2 %copy-start.12 = (f32[1,1,16,16384]{3,2,1,0:T(8,128)S(1)}, f32[1,1,16,16384]{3,2,1,0:T(8,128)}, u32[]{:S(2)}) copy-start(f32[1,1,16,16384]{3,2,1,0:T(8,128)} %stack.33) | copy-start | bytes 3145732
  232.1 6.2 %copy-start.13 = (f32[1,1,16,16384]{3,2,1,0:T(8,128)S(1)}, f32[1,1,16,16384]{3,2,1,0:T(8,128)}, u32[]{:S(2)}) copy-start(f32[1,1,16,16384]{3,2,1,0:T(8,128)} %stack.31) | copy-start | bytes 3145732
  232.1 6.2 %copy-start.14 = (f32[1,1,16,16384]{3,2,1,0:T(8,128)S(1)}, f32[1,1,16,16384]{3,2,1,0:T(8,128)}, u32[]{:S(2)}) copy-start(f32[1,1,16,16384]{3,2,1,0:T(8,128)} %stack.30) | copy-start | bytes 3145732
Sparse Core Ops, SparseCore 0:
  210.4 90.4 reduce-scatter.1
